TPU v7x, 256 devices: a whole 4x4x8 slice. The times are simulated.
256 devices in a mesh: row: 16 (over z, core), col: 16 (over x, y).
Axes of the slice: x: 4, y: 4, z: 8, core: 2. Of those that a mesh axis runs over, the one named last changes fastest.
Arguments:
- multipliers: float32 [256, 2, 16, 256], P(('row', 'col')), may hold values from -6 to 6
- residual: float32 [256, 2, 16, 256], P(('row', 'col')), may hold values from -18 to 18
- direction: float32 [256, 2, 16, 256], P(('row', 'col')), may hold values from -6 to 6
- energy_prev: float32 [16], replicated, may hold values from 262144 to 1048576
- hypersingular: bfloat16 [256, 1152, 1152], P(('row', 'col')), may hold values from -1 to 4, as said below
- double_layer: bfloat16 [256, 1152, 1152], P(('row', 'col')), may hold values from -0.1875 to 0.1875
- single_inverse: bfloat16 [256, 1152, 1152], P(('row', 'col')), may hold values from -1 to 4, as said below
- neumann_inverse: bfloat16 [256, 1152, 1152], P(('row', 'col')), may hold values from -1 to 4, as said below
- rigid_modes: float32 [256, 6, 1152], P(('row', 'col')), may hold values from -0.75 to 0.75
- coarse_inverse: float32 [1536, 1536], P(('row', 'col')), may hold values from -0.625 to 0.625
- face_index: int32 [256, 4, 256], P(('row', 'col')), may hold values from 0 to 1151, as said below
Outputs:
- multipliers_next: float32 [256, 2, 16, 256], P(('row', 'col'))
- residual_next: float32 [256, 2, 16, 256], P(('row', 'col'))
- direction_next: float32 [256, 2, 16, 256], P(('row', 'col'))
Inputs may be any that keep to these rules, and one draw needn't show every extreme that they name: For each patch the 1024 entries of face_index are distinct. `hypersingular`: each patch's matrix is symmetric positive definite. `single_inverse`: each patch's matrix is symmetric positive definite. `neumann_inverse`: each patch's matrix is symmetric positive definite.
All inputs are finite; a program needn't handle non-finite values.
Results may differ from a plain program's by a relative error of at most 0.0015.
Values sent between devices are 32-bit elements; how exact they have to be, the bound alone decides.
No kernel may reach another device: no remote copies, remote signals or barrier semaphores. Data moves between devices by JAX's collectives and lax.ppermute only.
A program may use at most 64 MiB of HBM per device.

v0:
```python
import jax
import jax.numpy as jnp
from jax import lax
from jax.sharding import PartitionSpec as P

NB = 1152
highest = lax.Precision.HIGHEST
contract_last = (((1,), (1,)), ((), ()))
contract_first = (((0,), (0,)), ((), ()))


def shifted(block, axis, distance):
    devices = range(lax.axis_size(axis))
    route = [((i - distance) % len(devices), i) for i in devices]
    return lax.ppermute(block, axis, route)


def spread_faces(values, face_where):
    from_left = shifted(values[0], "col", 1)
    from_below = shifted(values[1], "row", 1)
    pieces = jnp.concatenate([values[0], values[1], -from_left, -from_below], axis=1)
    return jnp.zeros((values.shape[1], NB), jnp.float32).at[:, face_where].set(pieces)


def jump_faces(vectors, face_where):
    face_width = face_where.shape[0] // 4
    picked = jnp.take(vectors, face_where, axis=1)
    from_right = shifted(picked[:, 2 * face_width : 3 * face_width], "col", -1)
    from_above = shifted(picked[:, 3 * face_width :], "row", -1)
    return jnp.stack(
        [picked[:, :face_width] - from_right, picked[:, face_width : 2 * face_width] - from_above]
    )


def project(values, face_where, rigid_local, coarse_rows):
    spread = spread_faces(values, face_where)
    partial_value = lax.dot_general(rigid_local, spread, contract_last, precision=highest)
    coarse_coef = jnp.dot(
        coarse_rows,
        lax.all_gather(partial_value, ("row", "col"), axis=0, tiled=True),
        precision=highest,
    )
    modes_back = lax.dot_general(coarse_coef, rigid_local, contract_first, precision=highest)
    correction = jump_faces(modes_back, face_where)
    return values - correction


def on_device(
    multipliers,
    residual,
    direction,
    energy_prev,
    hypersingular,
    double_layer,
    single_inverse,
    neumann_inverse,
    rigid_modes,
    coarse_inverse,
    face_index,
):
    face_where = face_index[0].reshape(-1)
    rigid_local = rigid_modes[0]
    hyper_local = hypersingular[0]
    double_local = double_layer[0]
    single_local = single_inverse[0]
    neumann_local = neumann_inverse[0]
    multipliers_now = multipliers[0]
    residual_now = residual[0]
    direction_now = direction[0]
    cases = residual_now.shape[1]
    projected = project(residual_now, face_where, rigid_local, coarse_inverse)
    rounded = spread_faces(projected, face_where).astype(jnp.bfloat16)
    lifted = (
        0.5 * rounded.astype(jnp.float32)
        + jnp.dot(rounded, double_local, preferred_element_type=jnp.float32)
    ).astype(jnp.bfloat16)
    weighed = jnp.dot(lifted, single_local, preferred_element_type=jnp.float32).astype(jnp.bfloat16)
    applied = (
        jnp.dot(rounded, hyper_local, preferred_element_type=jnp.float32)
        + 0.5 * weighed.astype(jnp.float32)
        + lax.dot_general(weighed, double_local, contract_last, preferred_element_type=jnp.float32)
    )
    energy_local = jnp.sum(rounded.astype(jnp.float32) * applied, axis=1)
    searched = project(jump_faces(applied, face_where), face_where, rigid_local, coarse_inverse)
    paired = spread_faces(jnp.concatenate([searched, direction_now], axis=1), face_where).astype(
        jnp.bfloat16
    )
    paired_applied = jnp.dot(paired, neumann_local, preferred_element_type=jnp.float32)
    paired_new = paired[:cases].astype(jnp.float32)
    paired_old = paired[cases:].astype(jnp.float32)
    applied_new = paired_applied[:cases]
    applied_old = paired_applied[cases:]
    energy = lax.psum(energy_local, ("row", "col"))
    step_ratio = energy / energy_prev
    spread_dir = paired_new + step_ratio[:, None] * paired_old
    applied_dir = applied_new + step_ratio[:, None] * applied_old
    curvature = lax.psum(jnp.sum(spread_dir * applied_dir, axis=1), ("row", "col"))
    step_size = energy / curvature
    direction_now = searched + step_ratio[None, :, None] * direction_now
    multipliers_now = multipliers_now + step_size[None, :, None] * direction_now
    corrected = project(
        jump_faces(applied_dir, face_where), face_where, rigid_local, coarse_inverse
    )
    residual_now = residual_now - step_size[None, :, None] * corrected
    return (multipliers_now[None], residual_now[None], direction_now[None])


def solution(mesh):
    return jax.shard_map(
        on_device,
        mesh=mesh,
        in_specs=(
            P(("row", "col"), None, None, None),
            P(("row", "col"), None, None, None),
            P(("row", "col"), None, None, None),
            P(),
            P(("row", "col"), None, None),
            P(("row", "col"), None, None),
            P(("row", "col"), None, None),
            P(("row", "col"), None, None),
            P(("row", "col"), None, None),
            P(("row", "col"), None),
            P(("row", "col"), None, None),
        ),
        out_specs=(
            P(("row", "col"), None, None, None),
            P(("row", "col"), None, None, None),
            P(("row", "col"), None, None, None),
        ),
        check_vma=False,
    )
```

profile of v0, /device:TPU:1, one launch (start us, length us, event | category | flops | bytes accessed | tf_op | source)
XLA Modules:
  0.0 625.8 jit_solution(15641244841059424459)
XLA Ops:
  0.7 0.9 slice_bitcast_fusion.3
  1.6 2.1 collective-permute-start
  3.7 2.5 collective-permute-start.1
  8.5 1.0 copy.82
  9.5 3.6 scatter_custom_fusion
  13.1 1.2 convolution_bitcast_fusion.2
  14.3 111.3 %all-gather = f32[256,6,16]{2,1,0:T(8,128)} all-gather(f32[1,6,16]{2,1,0:T(8,128)S(1)} %convolution_bitcast_fusion.2), channel_id=1, replica_groups=mesh['row'=16,'col'=16] {'row','col'}, dimensions={0}, use_global_device_ids=true | all-gather | bytes 98688 | tf_op jit(solution)/shard_map/all_gather | solution.py:40
  125.6 1.3 reshape.261
  127.5 1.1 fusion.53
  128.6 4.0 gather_fusion
  132.7 1.2 select_bitcast_fusion.2
  133.9 2.5 collective-permute-start.2
  136.4 2.2 collective-permute-done.2
  139.3 1.5 collective-permute-start.3
  141.5 2.4 collective-permute-done.3
  145.0 6.5 %collective-permute-done.4 = f32[16,256]{1,0:T(8,128)S(1)} collective-permute-done((f32[16,256]{1,0:T(8,128)S(1)}, f32[16,256]{1,0:T(8,128)S(1)}, u32[]{:S(2)}, u32[]{:S(2)}) %collective-permute-start.4) | collective-permute-done | bytes 16416 | tf_op jit(solution)/shard_map/ppermute | solution.py:15
  151.5 1.0 copy.86
  152.5 3.6 scatter_custom_fusion.1
  156.3 2.6 fusion.22
  159.6 0.9 copy-done.1
  160.6 1.7 fusion.41
  162.3 1.1 copy.88
  163.4 4.0 gather_fusion.1
  167.5 1.2 copy.89
  168.7 1.7 collective-permute-start.6
  170.4 1.1 collective-permute-done.6
  171.6 3.6 collective-permute-start.7
  176.1 5.6 collective-permute-done.8
  181.7 1.0 copy.90
  182.8 3.6 scatter_custom_fusion.2
  186.8 107.6 %all-gather.1 = f32[256,6,16]{2,1,0:T(8,128)} all-gather(f32[1,6,16]{2,1,0:T(8,128)S(1)} %convolution_bitcast_fusion.1), channel_id=1, replica_groups=mesh['row'=16,'col'=16] {'row','col'}, dimensions={0}, use_global_device_ids=true | all-gather | bytes 98688 | tf_op jit(solution)/shard_map/all_gather | solution.py:40
  294.4 1.3 reshape.263
  296.3 1.1 fusion.50
  297.4 4.0 gather_fusion.2
  301.4 1.2 select_bitcast_fusion.1
  302.7 2.5 collective-permute-start.10
  305.2 1.8 collective-permute-start.11
  307.1 2.4 collective-permute-done.11
  310.6 79.8 %psum.14 = f32[16]{0:T(128)S(1)} all-reduce(f32[16]{0:T(128)} %get-tuple-element.37), channel_id=1, replica_groups=mesh['row'=16,'col'=16] {'row','col'}, use_global_device_ids=true, to_apply=%region_3.5 | all-reduce | flops 16 | bytes 128 | tf_op jit(solution)/shard_map/psum | solution.py:93
  390.4 1.2 div.6
  391.7 1.0 copy.94
  392.7 3.6 scatter_custom_fusion.3
  396.5 2.3 fusion
  399.8 4.0 gather_fusion.3
  403.8 1.2 copy.99
  405.0 1.2 collective-permute-start.14
  406.3 1.4 collective-permute-done.14
  407.7 1.8 collective-permute-start.15
  409.5 1.3 collective-permute-done.15
  410.9 4.5 collective-permute-done.16
  415.5 1.0 copy.100
  416.5 3.6 scatter_custom_fusion.4
  420.6 108.0 %all-gather.2 = f32[256,6,16]{2,1,0:T(8,128)} all-gather(f32[1,6,16]{2,1,0:T(8,128)S(1)} %convolution_bitcast_fusion), channel_id=1, replica_groups=mesh['row'=16,'col'=16] {'row','col'}, dimensions={0}, use_global_device_ids=true | all-gather | bytes 98688 | tf_op jit(solution)/shard_map/all_gather | solution.py:40
  528.5 1.3 reshape.265
  530.4 1.1 fusion.47
  531.5 4.0 gather_fusion.4
  535.6 1.2 select_bitcast_fusion
  536.9 2.4 collective-permute-start.18
  539.3 1.9 collective-permute-done.18
  541.9 2.0 collective-permute-start.19
  544.0 1.6 copy.96
  546.2 76.4 %psum.15 = f32[16]{0:T(128)S(1)} all-reduce(f32[16]{0:T(128)} %get-tuple-element.12), channel_id=1, replica_groups=mesh['row'=16,'col'=16] {'row','col'}, use_global_device_ids=true, to_apply=%region_7.9 | all-reduce | flops 16 | bytes 128 | tf_op jit(solution)/shard_map/psum | solution.py:97
  623.2 0.9 fusion.37
  624.3 1.5 multiply_add_fusion
  (118 shorter events, 13.5 us)
Async XLA Ops:
  0.6 155.6 %copy-start = (bf16[1,1152,1152]{2,1,0:T(8,128)(2,1)S(1)}, bf16[1,1152,1152]{2,1,0:T(8,128)(2,1)}, u32[]{:S(2)}) copy-start(bf16[1,1152,1152]{2,1,0:T(8,128)(2,1)} %param.18) | copy-start | bytes 7962628
  0.6 126.3 %copy-start.4 = (f32[6,1536]{1,0:T(8,128)S(1)}, f32[6,1536]{1,0:T(8,128)}, u32[]{:S(2)}) copy-start(f32[6,1536]{1,0:T(8,128)} %param.22) | copy-start | bytes 110596
  1.6 6.9 %collective-permute-start = (f32[16,256]{1,0:T(8,128)S(1)}, f32[16,256]{1,0:T(8,128)S(1)}, u32[]{:S(2)}, u32[]{:S(2)}) collective-permute-start(f32[16,256]{1,0:T(8,128)S(1)} %get-tuple-element.34), channel_id=1, source_target_pairs={{15,0},{0,1},{1,2},{2,3},{3,4},{4,5},{5,6},{6,7},{7,8},{8,9},{9,10... | collective-permute-start | bytes 49160 | tf_op jit(solution)/shard_map/ppermute | solution.py:15
  3.7 4.8 collective-permute-start.1
  6.8 7.5 %copy-start.19 = (s32[1024,1]{0,1:T(1,128)}, s32[1024,1]{0,1:T(1,128)S(1)}, u32[]{:S(2)}) copy-start(s32[1024,1]{0,1:T(1,128)S(1)} %compare_select_fusion) | copy-start | bytes 12292
  8.5 119.0 %copy-start.2 = (f32[1,6,1152]{2,0,1:T(1,128)S(1)}, f32[1,6,1152]{2,0,1:T(1,128)}, u32[]{:S(2)}) copy-start(f32[1,6,1152]{2,0,1:T(1,128)} %param.21) | copy-start | bytes 82948
  126.9 17.0 %copy-start.5 = (f32[1,2,16,256]{3,2,1,0:T(8,128)S(1)}, f32[1,2,16,256]{3,2,1,0:T(8,128)}, u32[]{:S(2)}) copy-start(f32[1,2,16,256]{3,2,1,0:T(8,128)} %param.14) | copy-start | bytes 98308
  133.9 4.7 collective-permute-start.2
  139.3 4.6 collective-permute-start.3
  144.7 6.7 %collective-permute-start.4 = (f32[16,256]{1,0:T(8,128)S(1)}, f32[16,256]{1,0:T(8,128)S(1)}, u32[]{:S(2)}, u32[]{:S(2)}) collective-permute-start(f32[16,256]{1,0:T(8,128)S(1)} %get-tuple-element.32), channel_id=1, source_target_pairs={{15,0},{0,1},{1,2},{2,3},{3,4},{4,5},{5,6},{6,7},{7,8},{8,9},{9,10... | collective-permute-start | bytes 49160 | tf_op jit(solution)/shard_map/ppermute | solution.py:15
  144.8 6.6 %collective-permute-start.5 = (f32[16,256]{1,0:T(8,128)S(1)}, f32[16,256]{1,0:T(8,128)S(1)}, u32[]{:S(2)}, u32[]{:S(2)}) collective-permute-start(f32[16,256]{1,0:T(8,128)S(1)} %get-tuple-element.33), channel_id=1, source_target_pairs={{240,0},{0,16},{16,32},{32,48},{48,64},{64,80},{80,96},{96,112},{1... | collective-permute-start | bytes 49160 | tf_op jit(solution)/shard_map/ppermute | solution.py:15
  158.8 1.8 copy-start.1
  160.6 8.1 %copy-start.17 = (pred[1024]{0:T(1024)(128)(4,1)S(1)}, pred[1024]{0:T(1024)(128)(4,1)}, u32[]{:S(2)}) copy-start(pred[1024]{0:T(1024)(128)(4,1)} %compare_and_fusion) | copy-start | bytes 3076
  168.7 2.8 collective-permute-start.6
  171.6 10.1 %copy-start.6 = (f32[16,256]{1,0:T(8,128)}, f32[16,256]{1,0:T(8,128)S(1)}, u32[]{:S(2)}) copy-start(f32[16,256]{1,0:T(8,128)S(1)} %get-tuple-element.30) | copy-start | bytes 49156
  171.6 4.5 collective-permute-start.7
  175.2 6.5 %collective-permute-start.8 = (f32[16,256]{1,0:T(8,128)S(1)}, f32[16,256]{1,0:T(8,128)S(1)}, u32[]{:S(2)}, u32[]{:S(2)}) collective-permute-start(f32[16,256]{1,0:T(8,128)S(1)} %get-tuple-element.30), channel_id=1, source_target_pairs={{15,0},{0,1},{1,2},{2,3},{3,4},{4,5},{5,6},{6,7},{7,8},{8,9},{9,10... | collective-permute-start | bytes 49160 | tf_op jit(solution)/shard_map/ppermute | solution.py:15
  176.1 5.7 copy-start.9
  176.1 5.6 collective-permute-start.9
  296.2 14.2 %copy-start.7 = (f32[16,256]{1,0:T(8,128)S(1)}, f32[16,256]{1,0:T(8,128)}, u32[]{:S(2)}) copy-start(f32[16,256]{1,0:T(8,128)} %copy-done.6) | copy-start | bytes 49156
  296.2 14.2 %copy-start.10 = (f32[16,256]{1,0:T(8,128)S(1)}, f32[16,256]{1,0:T(8,128)}, u32[]{:S(2)}) copy-start(f32[16,256]{1,0:T(8,128)} %copy-done.9) | copy-start | bytes 49156
  296.3 14.2 %copy-start.16 = (f32[1,2,16,256]{3,2,1,0:T(8,128)S(1)}, f32[1,2,16,256]{3,2,1,0:T(8,128)}, u32[]{:S(2)}) copy-start(f32[1,2,16,256]{3,2,1,0:T(8,128)} %param.15) | copy-start | bytes 98308
  302.7 4.4 collective-permute-start.10
  305.2 4.4 collective-permute-start.11
  310.5 81.1 %collective-permute-start.12 = (f32[32,256]{1,0:T(8,128)S(1)}, f32[32,256]{1,0:T(8,128)S(1)}, u32[]{:S(2)}, u32[]{:S(2)}) collective-permute-start(f32[32,256]{1,0:T(8,128)S(1)} %get-tuple-element.28), channel_id=1, source_target_pairs={{15,0},{0,1},{1,2},{2,3},{3,4},{4,5},{5,6},{6,7},{7,8},{8,9},{9,10... | collective-permute-start | bytes 98312 | tf_op jit(solution)/shard_map/ppermute | solution.py:15
  310.6 81.0 %collective-permute-start.13 = (f32[32,256]{1,0:T(8,128)S(1)}, f32[32,256]{1,0:T(8,128)S(1)}, u32[]{:S(2)}, u32[]{:S(2)}) collective-permute-start(f32[32,256]{1,0:T(8,128)S(1)} %get-tuple-element.29), channel_id=1, source_target_pairs={{240,0},{0,16},{16,32},{32,48},{48,64},{64,80},{80,96},{96,112},{1... | collective-permute-start | bytes 98312 | tf_op jit(solution)/shard_map/ppermute | solution.py:15
  390.4 1.3 copy-start.21
  391.6 7.2 %copy-start.20 = (f32[16]{0:T(128)S(1)}, f32[16]{0:T(128)}, u32[]{:S(2)}) copy-start(f32[16]{0:T(128)} %div.6) | copy-start | bytes 196
  396.5 8.5 %copy-start.18 = (pred[1024]{0:T(1024)(128)(4,1)S(1)}, pred[1024]{0:T(1024)(128)(4,1)}, u32[]{:S(2)}) copy-start(pred[1024]{0:T(1024)(128)(4,1)} %compare_and_fusion) | copy-start | bytes 3076
  405.0 2.7 collective-permute-start.14
  407.7 7.8 %copy-start.12 = (f32[16,256]{1,0:T(8,128)}, f32[16,256]{1,0:T(8,128)S(1)}, u32[]{:S(2)}) copy-start(f32[16,256]{1,0:T(8,128)S(1)} %get-tuple-element.26) | copy-start | bytes 49156
  407.7 3.2 collective-permute-start.15
  409.5 5.9 collective-permute-start.16
  410.9 4.6 copy-start.14
  410.9 4.6 collective-permute-start.17
  530.4 15.1 %copy-start.3 = (f32[1,1,16,256]{2,3,1,0:T(8,128)S(1)}, f32[1,1,16,256]{2,3,1,0:T(8,128)}, u32[]{:S(2)}) copy-start(f32[1,1,16,256]{2,3,1,0:T(8,128)} %get-tuple-element.21) | copy-start | bytes 49156
  530.4 93.8 %copy-start.8 = (f32[16,256]{1,0:T(8,128)S(1)}, f32[16,256]{1,0:T(8,128)}, u32[]{:S(2)}) copy-start(f32[16,256]{1,0:T(8,128)} %copy-done.6) | copy-start | bytes 49156
  530.4 93.8 %copy-start.11 = (f32[16,256]{1,0:T(8,128)S(1)}, f32[16,256]{1,0:T(8,128)}, u32[]{:S(2)}) copy-start(f32[16,256]{1,0:T(8,128)} %copy-done.9) | copy-start | bytes 49156
  530.4 93.8 %copy-start.13 = (f32[16,256]{1,0:T(8,128)S(1)}, f32[16,256]{1,0:T(8,128)}, u32[]{:S(2)}) copy-start(f32[16,256]{1,0:T(8,128)} %copy-done.12) | copy-start | bytes 49156
  531.5 92.7 %copy-start.15 = (f32[16,256]{1,0:T(8,128)S(1)}, f32[16,256]{1,0:T(8,128)}, u32[]{:S(2)}) copy-start(f32[16,256]{1,0:T(8,128)} %copy-done.14) | copy-start | bytes 49156
  536.9 4.4 collective-permute-start.18
  541.9 81.3 %collective-permute-start.19 = (f32[16,256]{0,1:T(8,128)}, f32[16,256]{0,1:T(8,128)}, u32[]{:S(2)}, u32[]{:S(2)}) collective-permute-start(f32[16,256]{0,1:T(8,128)} %get-tuple-element.19), channel_id=1, source_target_pairs={{16,0},{32,16},{48,32},{64,48},{80,64},{96,80},{112,96},{128,112},... | collective-permute-start | bytes 49160 | tf_op jit(solution)/shard_map/ppermute | solution.py:15
where the time goes:
time: 627 us; the launch traced here: 626 us
  blocking collectives  483 us (77%)
  local copies, waits for them, and re-layouts  58 us (9%)
  waiting for transfers between devices  30.9 us (5%)
  starting transfers between devices  26 us (4%)
  matrix products  14.4 us (2%)
  other arithmetic  12.3 us (2%)
    all_gather x3, blocking collectives, project(): lax.all_gather(partial_value, ('row', 'col'), axis=0, tiled=True)  327 us
    psum x1, blocking collectives, on_device(): energy = lax.psum(energy_local, ('row', 'col'))  79.8 us
    psum x1, blocking collectives, on_device(): lax.psum(jnp.sum(spread_dir * applied_dir, axis=1), ('row', 'col'))  76.4 us
    ppermute x20, waiting for transfers between devices, shifted(): return lax.ppermute(block, axis, route)  30.9 us
    ppermute x20, starting transfers between devices, shifted(): return lax.ppermute(block, axis, route)  26 us
    gather x7, local copies, waits for them, and re-layouts, jump_faces(): picked = jnp.take(vectors, face_where, axis=1)  22.6 us
    scatter x7, local copies, waits for them, and re-layouts, spread_faces(): jnp.zeros((values.shape[1], NB), jnp.float32).at[:, face_where].set(pieces)  18.4 us
  transfers between devices with their start and end apart: 20, of which 13 were waited for; matrix products, arithmetic and copies ran while one was open for 1% of the time, Pallas kernels for 0%

commit v1 on v0

--- a/solution.py
+++ b/solution.py
@@ -37,7 +37,12 @@
     partial_value = lax.dot_general(rigid_local, spread, contract_last, precision=highest)
     coarse_coef = jnp.dot(
         coarse_rows,
-        lax.all_gather(partial_value, ("row", "col"), axis=0, tiled=True),
+        jnp.concatenate(
+            lax.all_to_all(
+                jnp.stack([partial_value] * lax.axis_size(("row", "col"))), ("row", "col"), 0, 0
+            ),
+            axis=0,
+        ),
         precision=highest,
     )
     modes_back = lax.dot_general(coarse_coef, rigid_local, contract_first, precision=highest)

time: 627 us -> 423 us (0.67)
  blocking collectives: 483 us -> 230 us
  waiting for transfers between devices: 30.9 us -> 60.1 us
  starting transfers between devices: 26 us -> 44 us
    all_gather x3 -> x0, blocking collectives: 327 us -> none  [project(): lax.all_gather(partial_value, ('row', 'col'), axis=0, tiled=True)]
    all_to_all x0 -> x2, blocking collectives: none -> 77.6 us  [project(): lax.all_to_all(jnp.stack([partial_value] * lax.axis_size(('row', 'col')))...]
    all_to_all x0 -> x1, waiting for transfers between devices: none -> 28.3 us  [project(): lax.all_to_all(jnp.stack([partial_value] * lax.axis_size(('row', 'col')))...]
    all_to_all x0 -> x1, starting transfers between devices: none -> 15.4 us  [project(): lax.all_to_all(jnp.stack([partial_value] * lax.axis_size(('row', 'col')))...]
  transfers between devices with their start and end apart: 20 -> 21, of which waited for: 13 -> 14; matrix products, arithmetic and copies ran while one was open for 1% -> 2% of each run, Pallas kernels for 0% -> 0%
where the time goes in v1:
time: 423 us; the launch traced here: 421 us
  blocking collectives  230 us (54%)
  waiting for transfers between devices  60.1 us (14%)
  local copies, waits for them, and re-layouts  59 us (14%)
  starting transfers between devices  44 us (10%)
  matrix products  14.4 us (3%)
  other arithmetic  12.3 us (3%)
    all_to_all x2, blocking collectives, project(): lax.all_to_all(jnp.stack([partial_value] * lax.axis_size(('row', 'col')))...  77.6 us
    psum x1, blocking collectives, on_device(): lax.psum(jnp.sum(spread_dir * applied_dir, axis=1), ('row', 'col'))  76.7 us
    psum x1, blocking collectives, on_device(): energy = lax.psum(energy_local, ('row', 'col'))  76.2 us
    ppermute x20, waiting for transfers between devices, shifted(): return lax.ppermute(block, axis, route)  31.8 us
    ppermute x20, starting transfers between devices, shifted(): return lax.ppermute(block, axis, route)  28.6 us
    all_to_all x1, waiting for transfers between devices, project(): lax.all_to_all(jnp.stack([partial_value] * lax.axis_size(('row', 'col')))...  28.3 us
    gather x7, local copies, waits for them, and re-layouts, jump_faces(): picked = jnp.take(vectors, face_where, axis=1)  22.5 us
    scatter x7, local copies, waits for them, and re-layouts, spread_faces(): jnp.zeros((values.shape[1], NB), jnp.float32).at[:, face_where].set(pieces)  18.4 us
  transfers between devices with their start and end apart: 21, of which 14 were waited for; matrix products, arithmetic and copies ran while one was open for 2% of the time, Pallas kernels for 0%

profile of v1, /device:TPU:1, one launch (start us, length us, event | category | flops | bytes accessed | tf_op | source)
XLA Modules:
  0.0 421.5 jit_solution(7339732432678487662)
XLA Ops:
  1.5 2.1 collective-permute-start
  3.6 2.5 collective-permute-start.1
  8.4 1.0 copy.82
  9.4 3.6 scatter_custom_fusion
  13.1 1.2 convolution_bitcast_fusion.2
  14.3 1.0 stack.48
  15.3 15.4 %all-to-all-start = ((f32[256,6,16]{2,1,0:T(8,128)}), f32[256,6,16]{2,1,0:T(8,128)}, u32[]{:S(2)}, u32[]{:S(2)}) async-start(f32[256,6,16]{2,1,0:T(8,128)} %stack.48), calls=%async_computation | async-start | bytes 2097152 | tf_op jit(solution)/shard_map/all_to_all | solution.py:41
  31.4 28.3 %all-to-all-done = f32[256,6,16]{2,1,0:T(8,128)} async-done(((f32[256,6,16]{2,1,0:T(8,128)}), f32[256,6,16]{2,1,0:T(8,128)}, u32[]{:S(2)}, u32[]{:S(2)}) %all-to-all-start) | async-done | bytes 98336 | tf_op jit(solution)/shard_map/all_to_all | solution.py:41
  59.6 1.3 reshape.190
  61.5 1.1 fusion.53
  62.6 4.0 gather_fusion
  66.6 1.2 select_bitcast_fusion.2
  67.9 2.7 collective-permute-start.2
  70.6 2.3 collective-permute-done.2
  73.6 1.9 collective-permute-start.3
  76.2 3.1 collective-permute-done.3
  80.1 1.1 collective-permute-start.4
  81.4 4.7 %collective-permute-done.4 = f32[16,256]{1,0:T(8,128)S(1)} collective-permute-done((f32[16,256]{1,0:T(8,128)S(1)}, f32[16,256]{1,0:T(8,128)S(1)}, u32[]{:S(2)}, u32[]{:S(2)}) %collective-permute-start.4) | collective-permute-done | bytes 16416 | tf_op jit(solution)/shard_map/ppermute | solution.py:15
  86.2 1.0 copy.86
  87.2 3.6 scatter_custom_fusion.1
  90.9 2.6 fusion.22
  95.3 1.7 fusion.41
  97.0 1.1 copy.88
  98.1 4.0 gather_fusion.1
  102.1 1.2 copy.89
  103.4 1.5 collective-permute-start.6
  104.9 1.1 collective-permute-done.6
  106.0 3.3 collective-permute-start.7
  110.2 5.6 %collective-permute-done.8 = f32[16,256]{1,0:T(8,128)S(1)} collective-permute-done((f32[16,256]{1,0:T(8,128)S(1)}, f32[16,256]{1,0:T(8,128)S(1)}, u32[]{:S(2)}, u32[]{:S(2)}) %collective-permute-start.8) | collective-permute-done | bytes 16416 | tf_op jit(solution)/shard_map/ppermute | solution.py:15
  115.9 1.0 copy.90
  116.9 3.6 scatter_custom_fusion.2
  121.0 39.2 %all_to_all.15 = f32[256,6,16]{2,1,0:T(8,128)} all-to-all(f32[256,6,16]{2,1,0:T(8,128)S(1)} %stack.55), channel_id=1, replica_groups=mesh['row'=16,'col'=16] {'row','col'}, dimensions={0} | all-to-all | bytes 196608 | tf_op jit(solution)/shard_map/all_to_all | solution.py:41
  160.2 1.3 reshape.191
  162.1 1.1 fusion.50
  163.2 4.0 gather_fusion.2
  167.2 1.2 select_bitcast_fusion.1
  168.5 2.7 collective-permute-start.10
  172.0 1.5 collective-permute-done.10
  173.5 2.1 collective-permute-done.11
  176.8 1.8 collective-permute-start.13
  178.6 76.2 %psum.14 = f32[16]{0:T(128)S(1)} all-reduce(f32[16]{0:T(128)} %get-tuple-element.37), channel_id=1, replica_groups=mesh['row'=16,'col'=16] {'row','col'}, use_global_device_ids=true, to_apply=%region_3.5 | all-reduce | flops 16 | bytes 128 | tf_op jit(solution)/shard_map/psum | solution.py:98
  254.8 1.2 div.6
  256.1 1.0 copy.94
  257.1 3.6 scatter_custom_fusion.3
  260.9 2.3 fusion
  264.2 4.0 gather_fusion.3
  268.2 1.2 copy.99
  269.5 1.2 collective-permute-start.14
  270.7 1.4 collective-permute-done.14
  272.2 1.8 collective-permute-start.15
  274.0 2.0 collective-permute-done.15
  276.0 3.8 collective-permute-done.16
  280.9 3.6 scatter_custom_fusion.4
  285.1 38.4 %all_to_all.16 = f32[256,6,16]{2,1,0:T(8,128)} all-to-all(f32[256,6,16]{2,1,0:T(8,128)S(1)} %stack.68), channel_id=1, replica_groups=mesh['row'=16,'col'=16] {'row','col'}, dimensions={0} | all-to-all | bytes 196608 | tf_op jit(solution)/shard_map/all_to_all | solution.py:41
  323.5 1.3 reshape.192
  325.3 1.1 fusion.47
  326.5 4.0 gather_fusion.4
  330.5 1.2 select_bitcast_fusion
  331.8 2.7 collective-permute-start.18
  334.4 2.3 collective-permute-done.18
  337.5 1.9 collective-permute-start.19
  339.3 1.6 copy.96
  341.6 76.7 %psum.15 = f32[16]{0:T(128)S(1)} all-reduce(f32[16]{0:T(128)} %get-tuple-element.12), channel_id=1, replica_groups=mesh['row'=16,'col'=16] {'row','col'}, use_global_device_ids=true, to_apply=%region_7.9 | all-reduce | flops 16 | bytes 128 | tf_op jit(solution)/shard_map/psum | solution.py:102
  420.0 1.5 multiply_add_fusion
  (122 shorter events, 18.9 us)
Async XLA Ops:
  0.6 90.3 %copy-start = (bf16[1,1152,1152]{2,1,0:T(8,128)(2,1)S(1)}, bf16[1,1152,1152]{2,1,0:T(8,128)(2,1)}, u32[]{:S(2)}) copy-start(bf16[1,1152,1152]{2,1,0:T(8,128)(2,1)} %param.18) | copy-start | bytes 7962628
  1.5 6.9 %collective-permute-start = (f32[16,256]{1,0:T(8,128)S(1)}, f32[16,256]{1,0:T(8,128)S(1)}, u32[]{:S(2)}, u32[]{:S(2)}) collective-permute-start(f32[16,256]{1,0:T(8,128)S(1)} %get-tuple-element.34), channel_id=1, source_target_pairs={{15,0},{0,1},{1,2},{2,3},{3,4},{4,5},{5,6},{6,7},{7,8},{8,9},{9,10... | collective-permute-start | bytes 49160 | tf_op jit(solution)/shard_map/ppermute | solution.py:15
  3.6 4.8 %collective-permute-start.1 = (f32[16,256]{1,0:T(8,128)S(1)}, f32[16,256]{1,0:T(8,128)S(1)}, u32[]{:S(2)}, u32[]{:S(2)}) collective-permute-start(f32[16,256]{1,0:T(8,128)S(1)} %get-tuple-element.35), channel_id=1, source_target_pairs={{240,0},{0,16},{16,32},{32,48},{48,64},{64,80},{80,96},{96,112},{1... | collective-permute-start | bytes 49160 | tf_op jit(solution)/shard_map/ppermute | solution.py:15
  6.8 52.8 %copy-start.19 = (s32[1024,1]{0,1:T(1,128)}, s32[1024,1]{0,1:T(1,128)S(1)}, u32[]{:S(2)}) copy-start(s32[1024,1]{0,1:T(1,128)S(1)} %compare_select_fusion) | copy-start | bytes 12292
  13.1 47.9 %copy-start.4 = (f32[6,1536]{1,0:T(8,128)S(1)}, f32[6,1536]{1,0:T(8,128)}, u32[]{:S(2)}) copy-start(f32[6,1536]{1,0:T(8,128)} %param.22) | copy-start | bytes 110596
  14.3 47.2 %copy-start.2 = (f32[1,6,1152]{2,0,1:T(1,128)S(1)}, f32[1,6,1152]{2,0,1:T(1,128)}, u32[]{:S(2)}) copy-start(f32[1,6,1152]{2,0,1:T(1,128)} %param.21) | copy-start | bytes 82948
  15.3 44.3 %all-to-all-start = ((f32[256,6,16]{2,1,0:T(8,128)}), f32[256,6,16]{2,1,0:T(8,128)}, u32[]{:S(2)}, u32[]{:S(2)}) async-start(f32[256,6,16]{2,1,0:T(8,128)} %stack.48), calls=%async_computation | async-start | bytes 2097152 | tf_op jit(solution)/shard_map/all_to_all | solution.py:41
  61.0 18.4 %copy-start.5 = (f32[1,2,16,256]{3,2,1,0:T(8,128)S(1)}, f32[1,2,16,256]{3,2,1,0:T(8,128)}, u32[]{:S(2)}) copy-start(f32[1,2,16,256]{3,2,1,0:T(8,128)} %param.14) | copy-start | bytes 98308
  67.9 5.0 %collective-permute-start.2 = (f32[16,256]{0,1:T(8,128)S(1)}, f32[16,256]{0,1:T(8,128)S(1)}, u32[]{:S(2)}, u32[]{:S(2)}) collective-permute-start(f32[16,256]{0,1:T(8,128)S(1)} %slice.139), channel_id=1, source_target_pairs={{1,0},{2,1},{3,2},{4,3},{5,4},{6,5},{7,6},{8,7},{9,8},{10,9},{11,1... | collective-permute-start | bytes 49160 | tf_op jit(solution)/shard_map/ppermute | solution.py:15
  73.6 5.6 %collective-permute-start.3 = (f32[16,256]{0,1:T(8,128)}, f32[16,256]{0,1:T(8,128)S(1)}, u32[]{:S(2)}, u32[]{:S(2)}) collective-permute-start(f32[16,256]{0,1:T(8,128)} %get-tuple-element.25), channel_id=1, source_target_pairs={{16,0},{32,16},{48,32},{64,48},{80,64},{96,80},{112,96},{128,112},... | collective-permute-start | bytes 49160 | tf_op jit(solution)/shard_map/ppermute | solution.py:15
  80.1 6.1 %collective-permute-start.4 = (f32[16,256]{1,0:T(8,128)S(1)}, f32[16,256]{1,0:T(8,128)S(1)}, u32[]{:S(2)}, u32[]{:S(2)}) collective-permute-start(f32[16,256]{1,0:T(8,128)S(1)} %get-tuple-element.32), channel_id=1, source_target_pairs={{15,0},{0,1},{1,2},{2,3},{3,4},{4,5},{5,6},{6,7},{7,8},{8,9},{9,10... | collective-permute-start | bytes 49160 | tf_op jit(solution)/shard_map/ppermute | solution.py:15
  81.2 5.0 %collective-permute-start.5 = (f32[16,256]{1,0:T(8,128)S(1)}, f32[16,256]{1,0:T(8,128)S(1)}, u32[]{:S(2)}, u32[]{:S(2)}) collective-permute-start(f32[16,256]{1,0:T(8,128)S(1)} %get-tuple-element.33), channel_id=1, source_target_pairs={{240,0},{0,16},{16,32},{32,48},{48,64},{64,80},{80,96},{96,112},{1... | collective-permute-start | bytes 49160 | tf_op jit(solution)/shard_map/ppermute | solution.py:15
  93.5 1.8 copy-start.1
  95.3 8.1 %copy-start.17 = (pred[1024]{0:T(1024)(128)(4,1)S(1)}, pred[1024]{0:T(1024)(128)(4,1)}, u32[]{:S(2)}) copy-start(pred[1024]{0:T(1024)(128)(4,1)} %compare_and_fusion) | copy-start | bytes 3076
  103.4 2.7 collective-permute-start.6
  106.0 9.8 %copy-start.6 = (f32[16,256]{1,0:T(8,128)}, f32[16,256]{1,0:T(8,128)S(1)}, u32[]{:S(2)}) copy-start(f32[16,256]{1,0:T(8,128)S(1)} %get-tuple-element.30) | copy-start | bytes 49156
  106.0 4.2 collective-permute-start.7
  109.4 6.5 %collective-permute-start.8 = (f32[16,256]{1,0:T(8,128)S(1)}, f32[16,256]{1,0:T(8,128)S(1)}, u32[]{:S(2)}, u32[]{:S(2)}) collective-permute-start(f32[16,256]{1,0:T(8,128)S(1)} %get-tuple-element.30), channel_id=1, source_target_pairs={{15,0},{0,1},{1,2},{2,3},{3,4},{4,5},{5,6},{6,7},{7,8},{8,9},{9,10... | collective-permute-start | bytes 49160 | tf_op jit(solution)/shard_map/ppermute | solution.py:15
  110.2 5.7 %copy-start.9 = (f32[16,256]{1,0:T(8,128)}, f32[16,256]{1,0:T(8,128)S(1)}, u32[]{:S(2)}) copy-start(f32[16,256]{1,0:T(8,128)S(1)} %slice_subtract_fusion.8) | copy-start | bytes 49156
  110.2 5.6 %collective-permute-start.9 = (f32[16,256]{1,0:T(8,128)S(1)}, f32[16,256]{1,0:T(8,128)S(1)}, u32[]{:S(2)}, u32[]{:S(2)}) collective-permute-start(f32[16,256]{1,0:T(8,128)S(1)} %slice_subtract_fusion.8), channel_id=1, source_target_pairs={{240,0},{0,16},{16,32},{32,48},{48,64},{64,80},{80,96},{96,112},{1... | collective-permute-start | bytes 49160 | tf_op jit(solution)/shard_map/ppermute | solution.py:15
  162.1 14.4 %copy-start.7 = (f32[16,256]{1,0:T(8,128)S(1)}, f32[16,256]{1,0:T(8,128)}, u32[]{:S(2)}) copy-start(f32[16,256]{1,0:T(8,128)} %copy-done.6) | copy-start | bytes 49156
  162.1 14.4 %copy-start.10 = (f32[16,256]{1,0:T(8,128)S(1)}, f32[16,256]{1,0:T(8,128)}, u32[]{:S(2)}) copy-start(f32[16,256]{1,0:T(8,128)} %copy-done.9) | copy-start | bytes 49156
  162.1 14.4 %copy-start.16 = (f32[1,2,16,256]{3,2,1,0:T(8,128)S(1)}, f32[1,2,16,256]{3,2,1,0:T(8,128)}, u32[]{:S(2)}) copy-start(f32[1,2,16,256]{3,2,1,0:T(8,128)} %param.15) | copy-start | bytes 98308
  168.5 5.0 %collective-permute-start.10 = (f32[16,256]{0,1:T(8,128)S(1)}, f32[16,256]{0,1:T(8,128)S(1)}, u32[]{:S(2)}, u32[]{:S(2)}) collective-permute-start(f32[16,256]{0,1:T(8,128)S(1)} %get-tuple-element.22), channel_id=1, source_target_pairs={{1,0},{2,1},{3,2},{4,3},{5,4},{6,5},{7,6},{8,7},{9,8},{10,9},{11,1... | collective-permute-start | bytes 49160 | tf_op jit(solution)/shard_map/ppermute | solution.py:15
  171.2 4.4 %collective-permute-start.11 = (f32[16,256]{0,1:T(8,128)S(1)}, f32[16,256]{0,1:T(8,128)S(1)}, u32[]{:S(2)}, u32[]{:S(2)}) collective-permute-start(f32[16,256]{0,1:T(8,128)S(1)} %get-tuple-element.23), channel_id=1, source_target_pairs={{16,0},{32,16},{48,32},{64,48},{80,64},{96,80},{112,96},{128,112},... | collective-permute-start | bytes 49160 | tf_op jit(solution)/shard_map/ppermute | solution.py:15
  176.5 79.5 %collective-permute-start.12 = (f32[32,256]{1,0:T(8,128)S(1)}, f32[32,256]{1,0:T(8,128)S(1)}, u32[]{:S(2)}, u32[]{:S(2)}) collective-permute-start(f32[32,256]{1,0:T(8,128)S(1)} %get-tuple-element.28), channel_id=1, source_target_pairs={{15,0},{0,1},{1,2},{2,3},{3,4},{4,5},{5,6},{6,7},{7,8},{8,9},{9,10... | collective-permute-start | bytes 98312 | tf_op jit(solution)/shard_map/ppermute | solution.py:15
  176.8 79.3 %collective-permute-start.13 = (f32[32,256]{1,0:T(8,128)S(1)}, f32[32,256]{1,0:T(8,128)S(1)}, u32[]{:S(2)}, u32[]{:S(2)}) collective-permute-start(f32[32,256]{1,0:T(8,128)S(1)} %get-tuple-element.29), channel_id=1, source_target_pairs={{240,0},{0,16},{16,32},{32,48},{48,64},{64,80},{80,96},{96,112},{1... | collective-permute-start | bytes 98312 | tf_op jit(solution)/shard_map/ppermute | solution.py:15
  254.8 1.3 copy-start.21
  256.1 7.2 %copy-start.20 = (f32[16]{0:T(128)S(1)}, f32[16]{0:T(128)}, u32[]{:S(2)}) copy-start(f32[16]{0:T(128)} %div.6) | copy-start | bytes 196
  260.9 8.5 %copy-start.18 = (pred[1024]{0:T(1024)(128)(4,1)S(1)}, pred[1024]{0:T(1024)(128)(4,1)}, u32[]{:S(2)}) copy-start(pred[1024]{0:T(1024)(128)(4,1)} %compare_and_fusion) | copy-start | bytes 3076
  269.5 2.7 collective-permute-start.14
  272.2 7.8 %copy-start.12 = (f32[16,256]{1,0:T(8,128)}, f32[16,256]{1,0:T(8,128)S(1)}, u32[]{:S(2)}) copy-start(f32[16,256]{1,0:T(8,128)S(1)} %get-tuple-element.26) | copy-start | bytes 49156
  272.2 3.9 collective-permute-start.15
  274.0 5.9 %collective-permute-start.16 = (f32[16,256]{1,0:T(8,128)S(1)}, f32[16,256]{1,0:T(8,128)S(1)}, u32[]{:S(2)}, u32[]{:S(2)}) collective-permute-start(f32[16,256]{1,0:T(8,128)S(1)} %get-tuple-element.26), channel_id=1, source_target_pairs={{15,0},{0,1},{1,2},{2,3},{3,4},{4,5},{5,6},{6,7},{7,8},{8,9},{9,10... | collective-permute-start | bytes 49160 | tf_op jit(solution)/shard_map/ppermute | solution.py:15
  276.0 3.9 copy-start.14
  276.0 3.9 collective-permute-start.17
  325.3 15.6 %copy-start.3 = (f32[1,1,16,256]{2,3,1,0:T(8,128)S(1)}, f32[1,1,16,256]{2,3,1,0:T(8,128)}, u32[]{:S(2)}) copy-start(f32[1,1,16,256]{2,3,1,0:T(8,128)} %get-tuple-element.21) | copy-start | bytes 49156
  325.3 94.6 %copy-start.8 = (f32[16,256]{1,0:T(8,128)S(1)}, f32[16,256]{1,0:T(8,128)}, u32[]{:S(2)}) copy-start(f32[16,256]{1,0:T(8,128)} %copy-done.6) | copy-start | bytes 49156
  325.3 94.6 %copy-start.11 = (f32[16,256]{1,0:T(8,128)S(1)}, f32[16,256]{1,0:T(8,128)}, u32[]{:S(2)}) copy-start(f32[16,256]{1,0:T(8,128)} %copy-done.9) | copy-start | bytes 49156
  325.3 94.6 %copy-start.13 = (f32[16,256]{1,0:T(8,128)S(1)}, f32[16,256]{1,0:T(8,128)}, u32[]{:S(2)}) copy-start(f32[16,256]{1,0:T(8,128)} %copy-done.12) | copy-start | bytes 49156
  326.5 93.5 %copy-start.15 = (f32[16,256]{1,0:T(8,128)S(1)}, f32[16,256]{1,0:T(8,128)}, u32[]{:S(2)}) copy-start(f32[16,256]{1,0:T(8,128)} %copy-done.14) | copy-start | bytes 49156
  331.8 5.0 %collective-permute-start.18 = (f32[16,256]{0,1:T(8,128)S(1)}, f32[16,256]{0,1:T(8,128)S(1)}, u32[]{:S(2)}, u32[]{:S(2)}) collective-permute-start(f32[16,256]{0,1:T(8,128)S(1)} %slice.163), channel_id=1, source_target_pairs={{1,0},{2,1},{3,2},{4,3},{5,4},{6,5},{7,6},{8,7},{9,8},{10,9},{11,1... | collective-permute-start | bytes 49160 | tf_op jit(solution)/shard_map/ppermute | solution.py:15
  337.5 81.5 %collective-permute-start.19 = (f32[16,256]{0,1:T(8,128)}, f32[16,256]{0,1:T(8,128)}, u32[]{:S(2)}, u32[]{:S(2)}) collective-permute-start(f32[16,256]{0,1:T(8,128)} %get-tuple-element.19), channel_id=1, source_target_pairs={{16,0},{32,16},{48,32},{64,48},{80,64},{96,80},{112,96},{128,112},... | collective-permute-start | bytes 49160 | tf_op jit(solution)/shard_map/ppermute | solution.py:15
